TPU v7x, 256 devices: a whole 4x4x8 slice. The times are simulated.
256 devices in a mesh: dp: 32 (over x, y, core), type: 8 (over z).
Axes of the slice: x: 4, y: 4, z: 8, core: 2. Of those that a mesh axis runs over, the one named last changes fastest.
Arguments:
- tokens: bfloat16 [32768, 4096], P(('dp', 'type')), may hold values from -6 to 6
- token_types: int32 [32768, 1], P(('dp', 'type')), may hold values from 0 to 7
- tile_mask: int32 [32, 8, 8], P('dp', 'type'), may hold values from 0 to 1, as said below
- queries: bfloat16 [32768, 4096], P(('dp', 'type')), may hold values from -60 to 60
- keys: bfloat16 [32768, 4096], P(('dp', 'type')), may hold values from -4 to 4
- gate_weight: bfloat16 [8, 4096, 7168], P('type', None, 'dp'), may hold values from -0.09375 to 0.09375
- up_weight: bfloat16 [8, 4096, 7168], P('type', None, 'dp'), may hold values from -0.09375 to 0.09375
- down_weight: bfloat16 [8, 7168, 4096], P('type', 'dp'), may hold values from -0.0625 to 0.0625
Outputs:
- expert_out: bfloat16 [32768, 4096], P(('dp', 'type'))
- attended: bfloat16 [32768, 4096], P(('dp', 'type'))
Inputs may be any that keep to these rules, and one draw needn't show every extreme that they name: `tile_mask`: every diagonal entry is 1.
All inputs are finite; a program needn't handle non-finite values.
Results may differ from a plain program's by a relative error of at most 0.02.
Values may be sent and summed in bfloat16 or wider, within the bound.
A program may use at most 128 MiB of HBM per device.

v0:
```python
import math

import jax
import jax.numpy as jnp
from jax import lax
from jax.sharding import PartitionSpec as P

HEAD = 128
EXP_CAP = 16


def on_device(tokens, token_types, tile_mask, queries, keys, gate_weight, up_weight, down_weight):
    n_type = lax.axis_size("type")
    my_index = lax.axis_index("type")
    tok_rows = tokens.shape[0]
    feat_width = tokens.shape[1]
    type_ids = jnp.arange(n_type, dtype=jnp.int32)
    slot_ids = jnp.arange(EXP_CAP, dtype=jnp.int32)
    own_types = token_types[:, 0]
    event_types = lax.all_gather(own_types, "type", axis=0, tiled=True)
    source_counts = jnp.sum(
        (event_types.reshape(n_type, tok_rows)[:, :, None] == type_ids[None, None, :]).astype(
            jnp.int32
        ),
        axis=1,
    )
    earlier = (type_ids < my_index).astype(jnp.int32)
    before_mine = jnp.sum(source_counts * earlier[:, None], axis=0)
    own_hot = (own_types[:, None] == type_ids[None, :]).astype(jnp.int32)
    own_rank = jnp.sum((jnp.cumsum(own_hot, axis=0) - own_hot) * own_hot, axis=1)
    own_event_rank = own_rank + jnp.sum(own_hot * before_mine[None, :], axis=1)
    kept = own_event_rank < EXP_CAP
    select = (
        (own_types[None, None, :] == type_ids[:, None, None])
        & (own_rank[None, None, :] == slot_ids[None, :, None])
        & kept[None, None, :]
    ).astype(jnp.bfloat16)
    outgoing = jnp.einsum("ejt,td->ejd", select, tokens, preferred_element_type=jnp.float32).astype(
        jnp.bfloat16
    )
    incoming = lax.all_to_all(outgoing, "type", split_axis=0, concat_axis=0, tiled=True)
    mine_flags = (event_types == my_index).astype(jnp.int32).reshape(n_type, tok_rows)
    counts = jnp.sum(mine_flags, axis=1)
    offsets = jnp.cumsum(counts) - counts
    compact = (
        (offsets[None, :, None] + slot_ids[None, None, :] == slot_ids[:, None, None])
        & (slot_ids[None, None, :] < counts[None, :, None])
    ).astype(jnp.bfloat16)
    packed = jnp.einsum(
        "psj,sjd->pd", compact, incoming, preferred_element_type=jnp.float32
    ).astype(jnp.bfloat16)
    gate_local = gate_weight[0]
    up_local = up_weight[0]
    down_local = down_weight[0]
    block_rows = lax.all_gather(packed, "dp", axis=0, tiled=True)
    gate_act = jnp.dot(block_rows, gate_local, preferred_element_type=jnp.float32)
    up_act = jnp.dot(block_rows, up_local, preferred_element_type=jnp.float32)
    hidden = (jax.nn.silu(gate_act) * up_act).astype(jnp.bfloat16)
    partial_terms = jnp.dot(hidden, down_local, preferred_element_type=jnp.float32)
    summed = lax.psum_scatter(
        partial_terms.astype(jnp.bfloat16), "dp", scatter_dimension=0, tiled=True
    )
    back_rows = jnp.einsum(
        "psj,pd->sjd", compact, summed, preferred_element_type=jnp.float32
    ).astype(jnp.bfloat16)
    returned = lax.all_to_all(back_rows, "type", split_axis=0, concat_axis=0, tiled=True)
    expert_out = jnp.einsum(
        "ejt,ejd->td", select, returned, preferred_element_type=jnp.float32
    ).astype(jnp.bfloat16)
    keys_all, values = (
        lax.all_gather(keys, "type", axis=0, tiled=True),
        lax.all_gather(expert_out, "type", axis=0, tiled=True),
    )
    mask_row = tile_mask[0, 0]
    key_tile = jnp.arange(n_type * tok_rows, dtype=jnp.int32) // tok_rows
    allowed = (
        jnp.sum(
            (key_tile[:, None] == type_ids[None, :]).astype(jnp.int32) * mask_row[None, :], axis=1
        )
        == 1
    )
    head_count = feat_width // HEAD
    query_heads = queries.reshape(tok_rows, head_count, HEAD)
    key_heads = keys_all.reshape(-1, head_count, HEAD)
    value_heads = values.reshape(-1, head_count, HEAD)
    scores = jnp.einsum(
        "qhd,khd->hqk", query_heads, key_heads, preferred_element_type=jnp.float32
    ) * (1.0 / math.sqrt(HEAD))
    masked = jnp.where(allowed[None, None, :], scores, -jnp.inf)
    row_max = jnp.max(masked, axis=-1, keepdims=True)
    weights = jnp.where(allowed[None, None, :], jnp.exp(masked - row_max), 0.0).astype(jnp.bfloat16)
    total_weight = jnp.sum(weights.astype(jnp.float32), axis=-1)
    attended = (
        jnp.einsum("hqk,khd->qhd", weights, value_heads, preferred_element_type=jnp.float32)
        / jnp.transpose(total_weight)[:, :, None]
    )
    return (expert_out, attended.reshape(tok_rows, feat_width).astype(jnp.bfloat16))


def solution(mesh):
    return jax.shard_map(
        on_device,
        mesh=mesh,
        in_specs=(
            P(("dp", "type"), None),
            P(("dp", "type"), None),
            P("dp", "type", None),
            P(("dp", "type"), None),
            P(("dp", "type"), None),
            P("type", None, "dp"),
            P("type", None, "dp"),
            P("type", "dp", None),
        ),
        out_specs=(P(("dp", "type"), None), P(("dp", "type"), None)),
        check_vma=False,
    )
```

profile of v0, /device:TPU:1, one launch (start us, length us, event | category | flops | bytes accessed | tf_op | source)
XLA Modules:
  0.0 370.8 jit_solution(6790468805835420968)
XLA Ops:
  8.0 16.5 %all-gather = s32[1024,1]{0,1:T(1,128)S(1)} all-gather(s32[128,1]{0,1:T(1,128)} %param.9), channel_id=2, replica_groups=mesh['dp'=32,'type'=8] {'type'}, dimensions={0}, use_global_device_ids=true | all-gather | bytes 4608 | tf_op jit(solution)/shard_map/all_gather | solution.py:20
  24.5 0.7 iota_compare_fusion.6
  25.2 0.7 fusion.32
  25.9 0.2 convert_reduce_fusion.1
  26.2 0.1 multiply_reduce_fusion
  26.2 0.2 reduce_window_sum.18
  26.4 0.8 select_reduce_fusion
  27.3 2.6 convolution_convert_fusion.2
  29.9 3.6 all-to-all-start
  33.5 0.1 reduce_sum.67
  33.7 0.2 reduce-window.8
  33.8 0.1 iota_compare_fusion.5
  33.9 0.1 iota_add_fusion
  34.0 24.9 %all-to-all-done = bf16[8,16,4096]{2,1,0:T(8,128)(2,1)S(1)} async-done(((bf16[8,16,4096]{2,1,0:T(8,128)(2,1)}), bf16[8,16,4096]{2,1,0:T(8,128)(2,1)S(1)}, u32[]{:S(2)}, u32[]{:S(2)}) %all-to-all-start) | async-done | bytes 1048608 | tf_op jit(solution)/shard_map/all_to_all | solution.py:41
  58.9 1.0 fusion.6
  60.0 51.5 %all-gather.5.cloned.1.call-done = bf16[512,4096]{1,0:T(8,128)(2,1)} async-done(((bf16[16,4096]{1,0:T(8,128)(2,1)}), bf16[512,4096]{1,0:T(8,128)(2,1)}) %all-gather.5.cloned.1.call-update) | async-done | bytes 4194320 | tf_op jit(solution)/shard_map/all_gather | solution.py:55
  111.4 4.2 %fusion.11 = f32[512,224]{0,1:T(8,128)S(1)} fusion(bf16[512,4096]{1,0:T(8,128)(2,1)} %all-gather.5.cloned.1.call-done, bf16[1,4096,224]{1,2,0:T(8,128)(2,1)} %param.13), kind=kOutput, calls=%fused_computation.20 | convolution fusion | flops 939524096 | bytes 6488064 | tf_op jit(solution)/shard_map/dot_general | solution.py:56
  115.7 7.5 %convolution_convert_fusion = bf16[512,4096]{1,0:T(8,128)(2,1)} fusion(bf16[1,224,4096]{2,1,0:T(8,128)(2,1)S(1)} %copy-done, bf16[512,4096]{1,0:T(8,128)(2,1)} %all-gather.5.cloned.1.call-done, bf16[1,4096,224]{1,2,0:T(8,128)(2,1)} %param.14, f32[512,224]{0,1:T(8,128)S(1)} %fusion.11), kind=kOutput, calls=%fused_computation.8 | convolution fusion | flops 1881833472 | bytes 12517376 | tf_op jit(solution)/shard_map/dot_general | solution.py:59
  123.2 0.0 all-gather.9.cloned.1.call-start
  123.3 1.3 copy.19
  124.6 0.0 all-gather.7.cloned.1.call-start
  124.7 86.4 %reduce-scatter.2.cloned.1.call-done = bf16[16,4096]{1,0:T(8,128)(2,1)} async-done(((bf16[512,4096]{1,0:T(8,128)(2,1)}), bf16[16,4096]{1,0:T(8,128)(2,1)}) %reduce-scatter.2.cloned.1.call-update) | async-done | bytes 131088 | tf_op jit(solution)/shard_map/reduce_scatter | solution.py:60
  211.0 1.4 convolution_convert_fusion.1
  212.4 33.6 %all_to_all.10 = bf16[8,16,4096]{2,1,0:T(8,128)(2,1)S(1)} all-to-all(bf16[8,16,4096]{2,1,0:T(8,128)(2,1)S(1)} %convolution_convert_fusion.1), channel_id=1, replica_groups=mesh['dp'=32,'type'=8] {'type'}, dimensions={0} | all-to-all | bytes 2097152 | tf_op jit(solution)/shard_map/all_to_all | solution.py:66
  246.0 1.5 fusion.5
  247.5 0.1 select_reduce_fusion.2
  247.7 11.4 %fusion.21 = f32[32,128,1024]{2,1,0:T(8,128)} fusion(bf16[1024,32,128]{0,2,1:T(8,128)(2,1)} %bitcast.58, bf16[128,4096]{1,0:T(8,128)(2,1)S(1)} %copy-done.2), kind=kOutput, calls=%fused_computation.24 | convolution fusion | flops 1073741824 | bytes 26214400 | tf_op jit(solution)/shard_map/qhd,khd->hqk/dot_general | solution.py:86
  259.1 18.0 %convert_reduce_fusion = (f32[32,128]{1,0:T(8,128)S(1)}, bf16[32,128,1024]{2,1,0:T(8,128)(2,1)}) fusion(f32[32,128,1024]{2,1,0:T(8,128)} %fusion.21, pred[1024]{0:T(1024)(128)(4,1)S(1)} %broadcast_compare_fusion), kind=kOutput, calls=%fused_computation.1 | output fusion | flops 37749760 | bytes 25183232 | tf_op jit(solution)/shard_map/sub | solution.py:91
  277.1 64.8 %all-gather.7.cloned.1.call-done = bf16[1024,4096]{1,0:T(8,128)(2,1)} async-done(((bf16[128,4096]{1,0:T(8,128)(2,1)}), bf16[1024,4096]{1,0:T(8,128)(2,1)}) %all-gather.7.cloned.1.call-update) | async-done | bytes 8388624 | tf_op jit(solution)/shard_map/all_gather | solution.py:72
  341.8 12.0 %copy.26 = bf16[1024,4096]{0,1:T(8,128)(2,1)} copy(bf16[1024,4096]{1,0:T(8,128)(2,1)} %all-gather.7.cloned.1.call-done) | data formatting | bytes 16777216 | tf_op jit(solution)/shard_map/reshape | solution.py:85
  353.8 8.2 %fusion.7 = bf16[128,32,128]{0,2,1:T(8,128)(2,1)S(1)} fusion(bf16[1024,32,128]{0,2,1:T(8,128)(2,1)} %bitcast.59, bf16[32,128,1024]{2,1,0:T(8,128)(2,1)} %get-tuple-element.11, f32[128,32]{0,1:T(8,128)S(1)} %bitcast.68), kind=kOutput, calls=%fused_computation.16 | convolution fusion | flops 1074790400 | bytes 17842176 | tf_op jit(solution)/shard_map/hqk,khd->qhd/dot_general | solution.py:94
  362.1 1.3 copy.23
  (24 shorter events, 0.2 us)
Async XLA Ops:
  8.0 107.6 %copy-start = (bf16[1,224,4096]{2,1,0:T(8,128)(2,1)S(1)}, bf16[1,224,4096]{2,1,0:T(8,128)(2,1)}, u32[]{:S(2)}) copy-start(bf16[1,224,4096]{2,1,0:T(8,128)(2,1)} %param.15) | copy-start | bytes 5505028
  29.9 28.9 %all-to-all-start = ((bf16[8,16,4096]{2,1,0:T(8,128)(2,1)}), bf16[8,16,4096]{2,1,0:T(8,128)(2,1)S(1)}, u32[]{:S(2)}, u32[]{:S(2)}) async-start(bf16[8,16,4096]{2,1,0:T(8,128)(2,1)} %convolution_convert_fusion.2), calls=%async_computation | async-start | bytes 2097152 | tf_op jit(solution)/shard_map/all_to_all | solution.py:41
  33.5 78.0 %all-gather.5.cloned.1.call-start = ((), (), s32[]{:S(2)}) async-start(), calls=%async_computation.3 | async-start | bytes 4325376 | tf_op jit(solution)/shard_map/all_gather | solution.py:55
  59.9 151.1 %reduce-scatter.2.cloned.1.call-start = ((), (), s32[]{:S(2)}) async-start(), calls=%async_computation.4 | async-start | bytes 4325376 | tf_op jit(solution)/shard_map/reduce_scatter | solution.py:60
  115.6 7.6 %copy-start.3 = (bf16[128,4096]{1,0:T(8,128)(2,1)S(1)}, bf16[128,4096]{1,0:T(8,128)(2,1)}, u32[]{:S(2)}) copy-start(bf16[128,4096]{1,0:T(8,128)(2,1)} %param.12) | copy-start | bytes 3145732
  123.2 124.4 %copy-start.4 = (s32[1,1,8]{2,1,0:T(1,128)S(1)}, s32[1,1,8]{2,1,0:T(1,128)}, u32[]{:S(2)}) copy-start(s32[1,1,8]{2,1,0:T(1,128)} %param.10) | copy-start | bytes 100
  123.2 124.5 %copy-start.2 = (bf16[128,4096]{1,0:T(8,128)(2,1)S(1)}, bf16[128,4096]{1,0:T(8,128)(2,1)}, u32[]{:S(2)}) copy-start(bf16[128,4096]{1,0:T(8,128)(2,1)} %param.11) | copy-start | bytes 3145732
  123.2 124.5 %all-gather.9.cloned.1.call-start = ((), (), s32[]{:S(2)}) async-start(), calls=%async_computation.6 | async-start | bytes 9437184 | tf_op jit(solution)/shard_map/all_gather | solution.py:71
  124.6 217.2 %all-gather.7.cloned.1.call-start = ((), (), s32[]{:S(2)}) async-start(), calls=%async_computation.5 | async-start | bytes 9437184 | tf_op jit(solution)/shard_map/all_gather | solution.py:72
  353.8 9.6 %copy-start.1 = (bf16[1,224,4096]{2,1,0:T(8,128)(2,1)S(1)}, bf16[1,224,4096]{2,1,0:T(8,128)(2,1)}, u32[]{:S(2)}) copy-start(bf16[1,224,4096]{2,1,0:T(8,128)(2,1)} %param.15) | copy-start | bytes 5505028
Sparse Core Ops, SparseCore 0:
  60.0 51.3 all-gather.4
  123.3 87.6 reduce-scatter.1
Sparse Core Ops, SparseCore 1:
  126.0 95.0 all-gather.8
  247.6 94.2 all-gather.6
where the time goes:
time: 371 us
  waiting for transfers between devices  228 us (61%)
  blocking collectives  50.2 us (14%)
  matrix products  37.9 us (10%)
  other arithmetic  21.2 us (6%)
  between operations  15.7 us (4%)
  local copies, waits for them, and re-layouts  14.6 us (4%)
  starting transfers between devices  3.73 us (1%)
    reduce_scatter x1, waiting for transfers between devices, on_device(): lax.psum_scatter(partial_terms.astype(jnp.bfloat16), 'dp', scatter_dimens...  86.4 us
    all_gather x1, waiting for transfers between devices, on_device(): lax.all_gather(expert_out, 'type', axis=0, tiled=True)  64.8 us
    all_gather x1, waiting for transfers between devices, on_device(): block_rows = lax.all_gather(packed, 'dp', axis=0, tiled=True)  51.5 us
    all_to_all x1, blocking collectives, on_device(): lax.all_to_all(back_rows, 'type', split_axis=0, concat_axis=0, tiled=True)  33.6 us
    all_to_all x1, waiting for transfers between devices, on_device(): lax.all_to_all(outgoing, 'type', split_axis=0, concat_axis=0, tiled=True)  24.9 us
    sub x1, other arithmetic, on_device(): masked - row_max  18 us
    all_gather x1, blocking collectives, on_device(): event_types = lax.all_gather(own_types, 'type', axis=0, tiled=True)  16.5 us
    reshape x1, local copies, waits for them, and re-layouts, on_device(): value_heads = values.reshape(-1, head_count, HEAD)  12 us
  transfers between devices with their start and end apart: 5, of which 4 were waited for; matrix products, arithmetic and copies ran while one was open for 9% of the time, Pallas kernels for 0%

commit v1 on v0

v1 whole, which is shorter than its diff:
```python
import math

import jax
import jax.numpy as jnp
from jax import lax
from jax.sharding import PartitionSpec as P

HEAD = 128
EXP_CAP = 16


def on_device(tokens, token_types, tile_mask, queries, keys, gate_weight, up_weight, down_weight):
    n_type = lax.axis_size("type")
    my_index = lax.axis_index("type")
    tok_rows = tokens.shape[0]
    feat_width = tokens.shape[1]
    type_ids = jnp.arange(n_type, dtype=jnp.int32)
    slot_ids = jnp.arange(EXP_CAP, dtype=jnp.int32)
    keys_all = lax.all_gather(keys, "type", axis=0, tiled=True)
    event_types = lax.all_gather(token_types[:, 0], "type", axis=0, tiled=True)
    hot = (event_types[None, :] == type_ids[:, None]).astype(jnp.int32)
    rank = jnp.cumsum(hot, axis=1) - hot
    place = (
        ((rank[:, None, :] == slot_ids[None, :, None]) & (hot[:, None, :] == 1))
        .astype(jnp.bfloat16)
        .reshape(n_type * EXP_CAP, n_type * tok_rows)
    )
    own_place = lax.dynamic_slice_in_dim(place, my_index * tok_rows, tok_rows, 1)
    contrib = jnp.dot(own_place, tokens, preferred_element_type=jnp.float32).astype(jnp.bfloat16)
    packed = lax.psum_scatter(contrib, "type", scatter_dimension=0, tiled=True)
    block_rows = lax.all_gather(packed, "dp", axis=0, tiled=True)
    gate_act = jnp.dot(block_rows, gate_weight[0], preferred_element_type=jnp.float32)
    up_act = jnp.dot(block_rows, up_weight[0], preferred_element_type=jnp.float32)
    hidden = (jax.nn.silu(gate_act) * up_act).astype(jnp.bfloat16)
    partial_terms = jnp.dot(hidden, down_weight[0], preferred_element_type=jnp.float32)
    summed = lax.psum_scatter(
        partial_terms.astype(jnp.bfloat16), "dp", scatter_dimension=0, tiled=True
    )
    slot_values = lax.all_gather(summed, "type", axis=0, tiled=True)
    expert_out = jnp.einsum(
        "pt,pd->td", own_place, slot_values, preferred_element_type=jnp.float32
    ).astype(jnp.bfloat16)
    mask_row = tile_mask[0, 0]
    allowed = jnp.repeat(mask_row == 1, tok_rows)
    head_count = feat_width // HEAD
    query_heads = queries.reshape(tok_rows, head_count, HEAD)
    key_heads = keys_all.reshape(-1, head_count, HEAD)
    value_heads = slot_values.reshape(-1, head_count, HEAD)
    scores = jnp.einsum(
        "qhd,khd->hqk", query_heads, key_heads, preferred_element_type=jnp.float32
    ) * (1.0 / math.sqrt(HEAD))
    masked = jnp.where(allowed[None, None, :], scores, -jnp.inf)
    row_max = jnp.max(masked, axis=-1, keepdims=True)
    weights = jnp.where(allowed[None, None, :], jnp.exp(masked - row_max), 0.0).astype(jnp.bfloat16)
    total_weight = jnp.sum(weights.astype(jnp.float32), axis=-1)
    slot_weights = jnp.einsum(
        "hqk,pk->hqp", weights, place, preferred_element_type=jnp.float32
    ).astype(jnp.bfloat16)
    attended = (
        jnp.einsum("hqp,phd->qhd", slot_weights, value_heads, preferred_element_type=jnp.float32)
        / jnp.transpose(total_weight)[:, :, None]
    )
    return (expert_out, attended.reshape(tok_rows, feat_width).astype(jnp.bfloat16))


def solution(mesh):
    return jax.shard_map(
        on_device,
        mesh=mesh,
        in_specs=(
            P(("dp", "type"), None),
            P(("dp", "type"), None),
            P("dp", "type", None),
            P(("dp", "type"), None),
            P(("dp", "type"), None),
            P("type", None, "dp"),
            P("type", None, "dp"),
            P("type", "dp", None),
        ),
        out_specs=(P(("dp", "type"), None), P(("dp", "type"), None)),
        check_vma=False,
    )
```

time: 371 us -> 383 us (1.032); the launches traced: 371 us -> 378 us
  waiting for transfers between devices: 228 us -> 284 us
  blocking collectives: 50.2 us -> 16.5 us
  local copies, waits for them, and re-layouts: 14.6 us -> 7.32 us
    all_gather x2, waiting for transfers between devices: 64.8 us -> 106 us  [the longest x1 99.5 us: on_device(): keys_all = lax.all_gather(keys, 'type', axis=0, tiled=True)]
    reduce_scatter x0 -> x1, waiting for transfers between devices: none -> 36.1 us  [on_device(): packed = lax.psum_scatter(contrib, 'type', scatter_dimension=0, tiled=True)]
    all_to_all x1 -> x0, blocking collectives: 33.6 us -> none  [on_device(): lax.all_to_all(back_rows, 'type', split_axis=0, concat_axis=0, tiled=True)]
    all_to_all x1 -> x0, waiting for transfers between devices: 24.9 us -> none  [on_device(): lax.all_to_all(outgoing, 'type', split_axis=0, concat_axis=0, tiled=True)]
    reshape x1, local copies, waits for them, and re-layouts: 12 us -> 2.26 us  [on_device(): value_heads = slot_values.reshape(-1, head_count, HEAD)]
    all_gather x1, waiting for transfers between devices: 51.5 us -> 57.5 us  [on_device(): block_rows = lax.all_gather(packed, 'dp', axis=0, tiled=True)]
    dot_general x7 -> x5, matrix products: 26.5 us -> 23.7 us  [the longest x1 7.96 us: on_device(): jnp.einsum('hqp,phd->qhd', slot_weights, value_heads, preferred_element_t...]
  transfers between devices with their start and end apart: 5 -> 5, of which waited for: 4 -> 5; matrix products, arithmetic and copies ran while one was open for 9% -> 8% of each run, Pallas kernels for 0% -> 0%
where the time goes in v1:
time: 383 us; the launch traced here: 378 us
  waiting for transfers between devices  284 us (74%)
  matrix products  35.1 us (9%)
  other arithmetic  20.7 us (5%)
  blocking collectives  16.5 us (4%)
  between operations  13.9 us (4%)
  local copies, waits for them, and re-layouts  7.32 us (2%)
    all_gather x1, waiting for transfers between devices, on_device(): keys_all = lax.all_gather(keys, 'type', axis=0, tiled=True)  99.5 us
    reduce_scatter x1, waiting for transfers between devices, on_device(): lax.psum_scatter(partial_terms.astype(jnp.bfloat16), 'dp', scatter_dimens...  84.7 us
    all_gather x1, waiting for transfers between devices, on_device(): block_rows = lax.all_gather(packed, 'dp', axis=0, tiled=True)  57.5 us
    reduce_scatter x1, waiting for transfers between devices, on_device(): packed = lax.psum_scatter(contrib, 'type', scatter_dimension=0, tiled=True)  36.1 us
    sub x1, other arithmetic, on_device(): masked - row_max  18 us
    all_gather x1, blocking collectives, on_device(): event_types = lax.all_gather(token_types[:, 0], 'type', axis=0, tiled=True)  16.5 us
    dot_general x1, matrix products, on_device(): jnp.einsum('qhd,khd->hqk', query_heads, key_heads, preferred_element_type...  11.4 us
    dot_general x1, matrix products, on_device(): jnp.einsum('hqp,phd->qhd', slot_weights, value_heads, preferred_element_t...  7.96 us
  transfers between devices with their start and end apart: 5, of which 5 were waited for; matrix products, arithmetic and copies ran while one was open for 8% of the time, Pallas kernels for 0%

profile of v1, /device:TPU:1, one launch (start us, length us, event | category | flops | bytes accessed | tf_op | source)
XLA Modules:
  0.0 378.2 jit_solution(15770409194891240785)
XLA Ops:
  7.2 0.0 reduce-scatter.3.cloned.1.call-start
  7.2 16.5 %all-gather = s32[1024,1]{0,1:T(1,128)S(1)} all-gather(s32[128,1]{0,1:T(1,128)} %param.9), channel_id=2, replica_groups=mesh['dp'=32,'type'=8] {'type'}, dimensions={0}, use_global_device_ids=true | all-gather | bytes 4608 | tf_op jit(solution)/shard_map/all_gather | solution.py:20
  23.7 0.1 eq.76
  23.9 2.3 reduce-window.6
  26.1 0.3 slice_reduce_fusion
  26.4 0.2 reduce-window.9
  26.6 0.1 add_bitcast_fusion
  26.7 0.2 fusion.22
  26.8 2.6 convolution_convert_fusion.2
  29.5 0.0 reduce-scatter.3.cloned.1.call-update
  29.5 0.0 all-gather.5.cloned.1.call-start
  29.5 36.1 %reduce-scatter.3.cloned.1.call-done = bf16[16,4096]{1,0:T(8,128)(2,1)} async-done(((bf16[128,4096]{1,0:T(8,128)(2,1)}), bf16[16,4096]{1,0:T(8,128)(2,1)}) %reduce-scatter.3.cloned.1.call-update) | async-done | bytes 131088 | tf_op jit(solution)/shard_map/reduce_scatter | solution.py:30
  65.6 0.0 all-gather.5.cloned.1.call-update
  65.6 0.0 reduce-scatter.5.cloned.1.call-start
  65.7 57.5 %all-gather.5.cloned.1.call-done = bf16[512,4096]{1,0:T(8,128)(2,1)} async-done(((bf16[16,4096]{1,0:T(8,128)(2,1)}), bf16[512,4096]{1,0:T(8,128)(2,1)}) %all-gather.5.cloned.1.call-update) | async-done | bytes 4194320 | tf_op jit(solution)/shard_map/all_gather | solution.py:31
  123.2 4.2 %fusion.9 = f32[512,224]{0,1:T(8,128)S(1)} fusion(bf16[512,4096]{1,0:T(8,128)(2,1)} %all-gather.5.cloned.1.call-done, bf16[1,4096,224]{1,2,0:T(8,128)(2,1)} %param.13), kind=kOutput, calls=%fused_computation.16 | convolution fusion | flops 939524096 | bytes 6488064 | tf_op jit(solution)/shard_map/dot_general | solution.py:32
  127.4 7.4 %convolution_convert_fusion = bf16[512,4096]{1,0:T(8,128)(2,1)} fusion(bf16[1,224,4096]{2,1,0:T(8,128)(2,1)S(1)} %copy-done, bf16[512,4096]{1,0:T(8,128)(2,1)} %all-gather.5.cloned.1.call-done, bf16[1,4096,224]{1,2,0:T(8,128)(2,1)} %param.14, f32[512,224]{0,1:T(8,128)S(1)} %fusion.9), kind=kOutput, calls=%fused_computation.8 | convolution fusion | flops 1881833472 | bytes 12517376 | tf_op jit(solution)/shard_map/dot_general | solution.py:35
  134.8 0.0 reduce-scatter.5.cloned.1.call-update
  134.9 0.0 all-gather.9.cloned.1.call-start
  134.9 2.3 copy.13
  137.2 0.0 all-gather.9.cloned.1.call-update
  137.3 0.2 all-gather.7.cloned.1.call-start
  137.5 0.1 broadcast_bitcast_fusion
  137.6 84.7 %reduce-scatter.5.cloned.1.call-done = bf16[16,4096]{1,0:T(8,128)(2,1)} async-done(((bf16[512,4096]{1,0:T(8,128)(2,1)}), bf16[16,4096]{1,0:T(8,128)(2,1)}) %reduce-scatter.5.cloned.1.call-update) | async-done | bytes 131088 | tf_op jit(solution)/shard_map/reduce_scatter | solution.py:36
  222.3 99.5 %all-gather.9.cloned.1.call-done = bf16[1024,4096]{0,1:T(8,128)(2,1)} async-done(((bf16[128,4096]{0,1:T(8,128)(2,1)}), bf16[1024,4096]{0,1:T(8,128)(2,1)}) %all-gather.9.cloned.1.call-update) | async-done | bytes 8388624 | tf_op jit(solution)/shard_map/all_gather | solution.py:19
  321.8 11.4 %fusion.19 = f32[32,128,1024]{2,1,0:T(8,128)} fusion(bf16[1024,32,128]{0,2,1:T(8,128)(2,1)} %bitcast.58, bf16[128,4096]{1,0:T(8,128)(2,1)S(1)} %copy-done.2), kind=kOutput, calls=%fused_computation.21 | convolution fusion | flops 1073741824 | bytes 26214400 | tf_op jit(solution)/shard_map/qhd,khd->hqk/dot_general | solution.py:49
  333.2 18.0 %convert_reduce_fusion = (f32[32,128]{1,0:T(8,128)S(1)}, bf16[32,128,1024]{2,1,0:T(8,128)(2,1)}) fusion(f32[32,128,1024]{2,1,0:T(8,128)} %fusion.19, pred[1024]{0:T(1024)(128)(4,1)S(1)} %broadcast_bitcast_fusion), kind=kOutput, calls=%fused_computation.1 | output fusion | flops 37749760 | bytes 25183232 | tf_op jit(solution)/shard_map/sub | solution.py:54
  351.2 6.6 %all-gather.7.cloned.1.call-done = bf16[128,4096]{1,0:T(8,128)(2,1)} async-done(((bf16[16,4096]{1,0:T(8,128)(2,1)}), bf16[128,4096]{1,0:T(8,128)(2,1)}) %all-gather.7.cloned.1.call-update) | async-done | bytes 1048592 | tf_op jit(solution)/shard_map/all_gather | solution.py:39
  357.7 2.3 copy.19
  360.0 8.0 %fusion.5 = bf16[128,32,128]{0,2,1:T(8,128)(2,1)} fusion(bf16[128,32,128]{0,2,1:T(8,128)(2,1)} %bitcast.59, bf16[32,128,1024]{2,1,0:T(8,128)(2,1)} %get-tuple-element.7, f32[128,32]{0,1:T(8,128)S(1)} %bitcast.65, pred[128,1024]{1,0:T(32,128)(4,1)S(1)} %fusion.22), kind=kOutput, calls=%fused_computation.12 | convolution fusion | flops 1209532416 | bytes 10633216 | tf_op jit(solution)/shard_map/hqp,phd->qhd/dot_general | solution.py:60
  368.0 2.3 copy.17
  370.2 1.5 convolution_convert_fusion.1
  (14 shorter events, 0.1 us)
Async XLA Ops:
  7.2 120.2 %copy-start = (bf16[1,224,4096]{2,1,0:T(8,128)(2,1)S(1)}, bf16[1,224,4096]{2,1,0:T(8,128)(2,1)}, u32[]{:S(2)}) copy-start(bf16[1,224,4096]{2,1,0:T(8,128)(2,1)} %param.15) | copy-start | bytes 5505028
  7.2 58.4 %reduce-scatter.3.cloned.1.call-start = ((), (), s32[]{:S(2)}) async-start(), calls=%async_computation.2 | async-start | bytes 1179648 | tf_op jit(solution)/shard_map/reduce_scatter | solution.py:30
  29.5 93.7 %all-gather.5.cloned.1.call-start = ((), (), s32[]{:S(2)}) async-start(), calls=%async_computation.3 | async-start | bytes 4325376 | tf_op jit(solution)/shard_map/all_gather | solution.py:31
  65.6 156.7 %reduce-scatter.5.cloned.1.call-start = ((), (), s32[]{:S(2)}) async-start(), calls=%async_computation.4 | async-start | bytes 4325376 | tf_op jit(solution)/shard_map/reduce_scatter | solution.py:36
  134.8 2.7 copy-start.3
  134.8 186.9 %copy-start.2 = (bf16[128,4096]{1,0:T(8,128)(2,1)S(1)}, bf16[128,4096]{1,0:T(8,128)(2,1)}, u32[]{:S(2)}) copy-start(bf16[128,4096]{1,0:T(8,128)(2,1)} %param.11) | copy-start | bytes 3145732
  134.9 186.9 %all-gather.9.cloned.1.call-start = ((), (), s32[]{:S(2)}) async-start(), calls=%async_computation.6 | async-start | bytes 9437184 | tf_op jit(solution)/shard_map/all_gather | solution.py:19
  137.3 220.5 %all-gather.7.cloned.1.call-start = ((), (), s32[]{:S(2)}) async-start(), calls=%async_computation.5 | async-start | bytes 1179648 | tf_op jit(solution)/shard_map/all_gather | solution.py:39
  360.0 10.2 %copy-start.1 = (bf16[128,4096]{1,0:T(8,128)(2,1)S(1)}, bf16[128,4096]{1,0:T(8,128)(2,1)}, u32[]{:S(2)}) copy-start(bf16[128,4096]{1,0:T(8,128)(2,1)} %all-gather.7.cloned.1.call-done) | copy-start | bytes 3145732
Sparse Core Ops, SparseCore 0:
  29.6 35.9 reduce-scatter.2
  68.2 54.9 all-gather.4
  135.0 87.2 reduce-scatter.4
  224.4 97.2 all-gather.8
  323.4 34.2 all-gather.6

commit v2 on v1

v2 whole, which is shorter than its diff:
```python
import math

import jax
import jax.numpy as jnp
from jax import lax
from jax.experimental import pallas as pl
from jax.experimental.pallas import tpu as pltpu
from jax.sharding import PartitionSpec as P

MESH = pl.DeviceIdType.MESH
BF = jnp.bfloat16
F32 = jnp.float32
HEAD = 128
CAP = 16
NZ = 8
NX = 4
TOK = 128
D = 4096
HALF = D // 2
FFB = 224
GRP = D // NZ
SCALE = 1.0 / math.sqrt(HEAD)
NEG = -1e30
N_SEM = 140
EARLY_KEYS = (1, 7)


def nt(a, b):
    return lax.dot_general(a, b, (((1,), (1,)), ((), ())), preferred_element_type=F32)


def tn(a, b):
    return lax.dot_general(a, b, (((0,), (0,)), ((), ())), preferred_element_type=F32)


def kernel(
    meta_in, tok_in, q_in, k_in, wg_in, wu_in, wd_in,
    oe_out, oa_out,
    mg, tok, qs, ka, qa, sa, mb, db, rb, sb, xf, wg, wu, wd, gacc, uacc, hid,
    ps, po, pr, s0, r0, s1, r1, yb, q0, z1, q1, vf, vv, kk, st, sr, wts, okm, oe, oa,
    ssem, rsem, lsem,
):
    z = lax.axis_index("type")
    dp = lax.axis_index("dp")
    core = dp % 2
    chip = dp // 2
    y = chip % NX
    x = chip // NX
    first = x * (1 - core) + y * core
    second = y * (1 - core) + x * core

    def plane(a, b):
        px = a * (1 - core) + b * core
        py = b * (1 - core) + a * core
        return {"dp": (px * NX + py) * 2 + core}

    sib = {"dp": dp + 1 - 2 * core}
    fp = plane((first + 1) % NX, second)
    fm = plane((first + NX - 1) % NX, second)
    sp = plane(first, (second + 1) % NX)
    sm = plane(first, (second + NX - 1) % NX)
    zp = {"type": (z + 1) % NZ}
    zm = {"type": (z + NZ - 1) % NZ}

    counter = [0]
    started = []

    def send(src, dst, device):
        at = counter[0]
        counter[0] += 1
        copy = pltpu.make_async_remote_copy(
            src_ref=src, dst_ref=dst, send_sem=ssem.at[at], recv_sem=rsem.at[at],
            device_id=device, device_id_type=MESH,
        )
        copy.start()
        started.append(copy)
        return copy

    locals_at = [0]

    def fetch(src, dst):
        copy = pltpu.make_async_copy(src, dst, lsem.at[locals_at[0]])
        locals_at[0] += 1
        copy.start()
        return copy

    def cols(i, width):
        return pl.ds(pl.multiple_of(i * width, width), width)

    get_meta = fetch(meta_in, mg.at[z])
    get_tok = fetch(tok_in, tok)
    get_k = fetch(k_in.at[:, cols(z, GRP)], ka.at[z])
    get_q = fetch(q_in.at[:, cols(z, GRP)], qa.at[z])
    get_qs = fetch(q_in, qs)
    get_w = [
        fetch(wg_in.at[0], wg),
        fetch(wu_in.at[0], wu),
        fetch(wd_in.at[0, :, pl.ds(0, HALF)], wd.at[0]),
        fetch(wd_in.at[0, :, pl.ds(HALF, HALF)], wd.at[1]),
    ]

    barrier = pltpu.get_barrier_semaphore()
    peers = [{"type": (z + d) % NZ} for d in range(1, NZ)] + [sib, fp, fm, sp, sm]
    for peer in peers:
        pl.semaphore_signal(barrier, inc=1, device_id=peer, device_id_type=MESH)
    pl.semaphore_wait(barrier, len(peers))

    get_meta.wait()
    meta_copies = [send(mg.at[z], mg.at[z], {"type": (z + d) % NZ}) for d in range(1, NZ)]

    def send_slice(src, dst, d):
        to = (z + d) % NZ
        return send(src.at[:, cols(to, GRP)], dst.at[z], {"type": to})

    key_copies = [send_slice(k_in, ka, d) for d in EARLY_KEYS]

    for copy in meta_copies:
        copy.wait_recv()

    expert = lax.broadcasted_iota(jnp.int32, (CAP, TOK), 0)
    hot = [jnp.broadcast_to(mg[s, 0:1, :], (CAP, TOK)) == expert for s in range(NZ)]
    hot_rows = jnp.concatenate([h.astype(F32) for h in hot], axis=0).astype(BF)
    row = lax.broadcasted_iota(jnp.int32, (TOK, 2 * TOK), 0)
    col = lax.broadcasted_iota(jnp.int32, (TOK, 2 * TOK), 1)
    upper = jnp.where((row < col) | (col >= TOK), 1.0, 0.0).astype(BF)
    sums = jnp.dot(hot_rows, upper, preferred_element_type=F32)
    offset = jnp.zeros((CAP, TOK), F32)
    ranks = []
    for s in range(NZ):
        part = sums[s * CAP : (s + 1) * CAP]
        rank = part[:, :TOK] + offset
        ranks.append(jnp.where(hot[s], jnp.minimum(rank, 31.0), 64.0))
        offset = offset + part[:, TOK:]
    rank_rows = jnp.concatenate(ranks, axis=1).astype(BF)
    slot = lax.broadcasted_iota(jnp.int32, (TOK, CAP), 0)
    of_expert = lax.broadcasted_iota(jnp.int32, (TOK, CAP), 1)
    spread = jnp.where(slot // CAP == of_expert, 1.0, 0.0).astype(BF)
    rank_of = jnp.dot(spread, rank_rows, preferred_element_type=F32)
    wanted = (lax.broadcasted_iota(jnp.int32, (TOK, TOK), 0) % CAP).astype(F32)
    for s in range(NZ):
        place = jnp.where(rank_of[:, s * TOK : (s + 1) * TOK] == wanted, 1.0, 0.0)
        sa[s] = place.astype(BF)

    get_tok.wait()
    mine = sa[z]
    for h in range(2):
        placed = jnp.dot(mine, tok[:, h * HALF : (h + 1) * HALF], preferred_element_type=F32)
        db[h] = placed.astype(BF).reshape(NZ, CAP, HALF)
    arriving = {}
    for step in range(4):
        for h in range(2):
            for way in range(2):
                begin = 0 if h == way else 1
                if step < begin:
                    continue
                far = 4 - step
                target = (z + far) % NZ if way == 0 else (z + NZ - far) % NZ
                if step == begin:
                    src = db.at[h, target]
                else:
                    arriving[h, way].wait_recv()
                    sb[way, h, step - 1] = db[h, target] + rb[way, h, step - 1]
                    src = sb.at[way, h, step - 1]
                arriving[h, way] = send(src, rb.at[way, h, step], zp if way == 0 else zm)

    key_copies += [send_slice(k_in, ka, d) for d in range(1, NZ) if d not in EARLY_KEYS]
    query_copies = [send_slice(q_in, qa, d) for d in range(1, NZ)]

    mask_rows = jnp.concatenate([mg[s, 1:2, :] for s in range(NZ)], axis=0)
    for j in range(NZ):
        mb[j] = jnp.broadcast_to(mask_rows[:, j : j + 1], (NZ, TOK)).astype(F32)

    for h in range(2):
        arriving[h, 0].wait_recv()
        arriving[h, 1].wait_recv()
        xf[h, second, first, core] = db[h, z] + rb[0, h, 3] + rb[1, h, 3]

    def own_row(h):
        return send(xf.at[h, second, first, core], xf.at[h, first, second, core], sib)

    row_a = own_row(1 - core)
    row_b = own_row(core)
    row_a.wait_recv()

    def unit(b, a):
        return xf.at[core, b, a]

    def to_sibling(b, a):
        return send(unit(b, a), xf.at[core, a, b], sib)

    def move(ref, device):
        return send(ref, ref, device)

    from_sib = []
    a_minus, a_plus, a_far = (first + NX - 1) % NX, (first + 1) % NX, (first + 2) % NX
    b_minus, b_plus, b_far = (second + NX - 1) % NX, (second + 1) % NX, (second + 2) % NX
    near_p = move(unit(second, first), fp)
    near_m = move(unit(second, first), fm)
    beside = [(first, move(unit(second, first), sp), move(unit(second, first), sm))]
    near_p.wait_recv()
    far_p = move(xf.at[core, second, a_minus, 0], fp)
    beside.append((a_minus, move(unit(second, a_minus), sp), move(unit(second, a_minus), sm)))
    from_sib.append(to_sibling(second, a_minus))
    near_m.wait_recv()
    far_m = move(xf.at[core, second, a_plus, 1], fm)
    beside.append((a_plus, move(unit(second, a_plus), sp), move(unit(second, a_plus), sm)))
    from_sib.append(to_sibling(second, a_plus))
    opposite = []

    def relay(entry):
        a, up, down = entry
        up.wait_recv()
        half_p = move(xf.at[core, b_minus, a, 0], sp)
        from_sib.append(to_sibling(b_minus, a))
        down.wait_recv()
        half_m = move(xf.at[core, b_plus, a, 1], sm)
        from_sib.append(to_sibling(b_plus, a))
        opposite.append((a, half_p, half_m))

    relay(beside[0])
    far_p.wait_recv()
    far_m.wait_recv()
    beside.append((a_far, move(unit(second, a_far), sp), move(unit(second, a_far), sm)))
    from_sib.append(to_sibling(second, a_far))

    def finish(entry):
        a, half_p, half_m = entry
        half_p.wait_recv()
        half_m.wait_recv()
        from_sib.append(to_sibling(b_far, a))

    for n in range(1, 4):
        relay(beside[n])
        finish(opposite[n - 1])
    finish(opposite[3])
    row_b.wait_recv()
    for copy in get_w:
        copy.wait()
    for copy in from_sib:
        copy.wait_recv()

    gacc[...] = jnp.zeros_like(gacc)
    uacc[...] = jnp.zeros_like(uacc)

    def up_step(k, carry):
        rows = xf[k // 4, :, :, :, :, cols(k % 4, 512)].reshape(512, 512)
        gacc[...] += jnp.dot(rows, wg[cols(k, 512), :], preferred_element_type=F32)
        uacc[...] += jnp.dot(rows, wu[cols(k, 512), :], preferred_element_type=F32)
        return carry

    lax.fori_loop(0, 8, up_step, 0)
    gate = gacc[...]
    hid[...] = (gate / (1.0 + jnp.exp(-gate)) * uacc[...]).astype(BF)

    def down_step(half, out):
        def step(n, carry):
            part = jnp.dot(hid[...], wd[half, :, cols(n, 512)], preferred_element_type=F32)
            out[:, :, :, :, cols(n, 512)] = part.astype(BF).reshape(NX, NX, 2, CAP, 512)
            return carry

        lax.fori_loop(0, 4, step, 0)

    down_step(1 - core, ps)
    shares = {}
    for name, a in (("far", a_far), ("plus", a_plus), ("minus", a_minus), ("own", first)):
        shares[name] = send(ps.at[:, a], pr.at[a], sib)
    down_step(core, po)

    def both(b, a):
        return po[b, a].astype(F32) + pr[b, a].astype(F32)

    shares["far"].wait_recv()
    for a in range(4):
        s0[a] = both(b_far, a).astype(BF)
        if a == 1:
            hop_p = send(s0.at[pl.ds(0, 2)], r0.at[0], sp)
    hop_m = send(s0.at[pl.ds(2, 2)], r0.at[1], sm)
    shares["plus"].wait_recv()
    for a in (2, 3):
        s1[0, a] = both(b_plus, a).astype(BF)
    last = [send(s1.at[0, pl.ds(2, 2)], r1.at[0, pl.ds(2, 2)], sp)]
    shares["minus"].wait_recv()
    for a in (0, 1):
        s1[1, a] = both(b_minus, a).astype(BF)
    last.append(send(s1.at[1, pl.ds(0, 2)], r1.at[1, pl.ds(0, 2)], sm))
    hop_p.wait_recv()
    for a in (0, 1):
        s1[0, a] = (both(b_plus, a) + r0[0, a].astype(F32)).astype(BF)
    last.append(send(s1.at[0, pl.ds(0, 2)], r1.at[0, pl.ds(0, 2)], sp))
    hop_m.wait_recv()
    for a in (2, 3):
        s1[1, a] = (both(b_minus, a) + r0[1, a - 2].astype(F32)).astype(BF)
    last.append(send(s1.at[1, pl.ds(2, 2)], r1.at[1, pl.ds(2, 2)], sm))

    shares["own"].wait_recv()
    for copy in last:
        copy.wait_recv()

    def summed(a):
        return both(second, a) + r1[0, a].astype(F32) + r1[1, a].astype(F32)

    yb[0] = summed(a_far).astype(BF)
    end_p = send(yb.at[0, 0], q0.at[0], fp)
    end_m = send(yb.at[0, 1], q0.at[1], fm)
    plus = summed(a_plus)
    z1[0, 1] = plus[1].astype(BF)
    ends = [send(z1.at[0, 1], q1.at[0, 1], fp)]
    minus = summed(a_minus)
    z1[1, 0] = minus[0].astype(BF)
    ends.append(send(z1.at[1, 0], q1.at[1, 0], fm))
    end_p.wait_recv()
    z1[0, 0] = (plus[0] + q0[0].astype(F32)).astype(BF)
    ends.append(send(z1.at[0, 0], q1.at[0, 0], fp))
    end_m.wait_recv()
    z1[1, 1] = (minus[1] + q0[1].astype(F32)).astype(BF)
    ends.append(send(z1.at[1, 1], q1.at[1, 1], fm))
    yb[1] = summed(first).astype(BF)
    for copy in ends:
        copy.wait_recv()

    def whole(event):
        return (
            yb[1, event].astype(F32) + q1[0, event].astype(F32) + q1[1, event].astype(F32)
        ).astype(BF)

    vf[...] = whole(1 - core)
    other = send(vf, vv.at[core, z], sib)
    vv[core, z] = whole(core)

    class Ring:
        def __init__(self, ref, longer):
            self.ref = ref
            self.longer = longer
            self.up = send(ref(z), ref(z), zp)
            self.down = send(ref(z), ref(z), zm)
            self.step = 1

        def relay(self):
            n = self.step
            self.step += 1
            if n < 4 or self.longer != "down":
                self.up.wait_recv()
            if n < 4 or self.longer != "up":
                self.down.wait_recv()
            if n >= 4:
                return
            below, above = (z + NZ - n) % NZ, (z + n) % NZ
            if n < 3 or self.longer == "up":
                self.up = send(self.ref(below), self.ref(below), zp)
            elif self.longer == "both":
                self.up = send(self.ref(below, 0), self.ref(below, 0), zp)
            if n < 3 or self.longer == "down":
                self.down = send(self.ref(above), self.ref(above), zm)
            elif self.longer == "both":
                self.down = send(self.ref(above, 1), self.ref(above, 1), zm)

    rings = [Ring(lambda e: vv.at[core, e], "up")]
    other.wait_recv()
    rings.append(Ring(lambda e: vv.at[1 - core, e], "down"))

    get_k.wait()
    for copy in key_copies:
        copy.wait_recv()
    kept = jnp.dot(sa[0], ka[0], preferred_element_type=F32)
    for s in range(1, NZ):
        kept += jnp.dot(sa[s], ka[s], preferred_element_type=F32)
    kk[z] = kept.astype(BF).reshape(2, TOK // 2, GRP)
    rings.append(
        Ring(lambda e, half=None: kk.at[e] if half is None else kk.at[e, half], "both")
    )

    get_q.wait()
    for copy in query_copies:
        copy.wait_recv()

    def attend(n, carry):
        i, h = n // 4, n % 4
        query = qa[i, :, cols(h, HEAD)]
        top = jnp.full((1, TOK), NEG, F32)
        tiles = []
        for j in range(NZ):
            s = nt(ka[j, :, cols(h, HEAD)], query)
            s = jnp.where(mb[j, pl.ds(i, 1), :] > 0.5, s, NEG)
            top = jnp.maximum(top, jnp.max(s, axis=0, keepdims=True))
            tiles.append(s)
        top = top * SCALE
        total = jnp.zeros((1, TOK), F32)
        for s in tiles:
            w = jnp.exp(s * SCALE - top).astype(BF).astype(F32)
            total += jnp.sum(w, axis=0, keepdims=True)
        st[i, pl.ds(h, 1), :] = top
        st[i, pl.ds(h + 4, 1), :] = total
        return carry

    lax.fori_loop(0, 12, attend, 0)
    for ring in rings:
        ring.relay()
    lax.fori_loop(12, 22, attend, 0)
    for ring in rings:
        ring.relay()
    lax.fori_loop(22, 32, attend, 0)
    stat_copies = []
    for d in range(1, NZ):
        to = (z + d) % NZ
        stat_copies.append(send(st.at[to], sr.at[z], {"type": to}))
    sr[z] = st[z]
    for ring in rings:
        ring.relay()

    open_slots = jnp.zeros((TOK, TOK), F32)
    for s in range(NZ):
        open_slots += sa[s].astype(F32) * mb[s, pl.ds(z, 1), :]
    okm[...] = jnp.broadcast_to(jnp.sum(open_slots, axis=1, keepdims=True), (TOK, TOK))

    get_qs.wait()
    for copy in stat_copies:
        copy.wait_recv()
    rings[2].relay()

    def weigh(g, carry):
        keys = kk[g].reshape(TOK, GRP)
        query = qs[:, cols(g, GRP)]
        for h in range(4):
            at = slice(h * HEAD, (h + 1) * HEAD)
            s = nt(keys[:, at], query[:, at]) * SCALE - sr[g, h : h + 1, :]
            wts[g * 4 + h] = jnp.where(okm[...] > 0.5, jnp.exp(s), 0.0).astype(BF)
        return carry

    lax.fori_loop(0, NZ, weigh, 0)
    stats = sr[...].reshape(NZ * 8, TOK)
    inverse = 1.0 / jnp.concatenate([stats, stats], axis=0).T
    rings[0].relay()
    rings[1].relay()

    for h in range(2):
        values = vv[h].reshape(TOK, HALF)
        oe[:, h * HALF : (h + 1) * HALF] = tn(sa[z], values).astype(BF)
    put_e = fetch(oe, oe_out)
    for head in range(32):
        h, at = head // 16, (head % 16) * HEAD
        values = vv[h, :, :, at : at + HEAD].reshape(TOK, HEAD)
        column = (head // 4) * 8 + 4 + head % 4
        mixed = tn(wts[head], values) * inverse[:, column : column + 1]
        oa[:, head * HEAD : (head + 1) * HEAD] = mixed.astype(BF)
    put_a = fetch(oa, oa_out)
    for copy in started:
        copy.wait_send()
    put_e.wait()
    put_a.wait()


def on_device(tokens, token_types, tile_mask, queries, keys, gate_weight, up_weight, down_weight):
    meta = jnp.concatenate(
        [
            token_types.reshape(1, TOK),
            jnp.pad(tile_mask.reshape(1, NZ), ((0, 0), (0, TOK - NZ))),
            jnp.zeros((6, TOK), jnp.int32),
        ],
        axis=0,
    )
    anywhere = pl.BlockSpec(memory_space=pl.ANY)

    def vmem(*shape, dtype=BF):
        return pltpu.VMEM(shape, dtype)

    return pl.pallas_call(
        kernel,
        out_shape=[jax.ShapeDtypeStruct((TOK, D), BF)] * 2,
        in_specs=[anywhere] * 7,
        out_specs=[anywhere] * 2,
        scratch_shapes=[
            vmem(NZ, 8, TOK, dtype=jnp.int32),
            vmem(TOK, D),
            vmem(TOK, D),
            vmem(NZ, TOK, GRP),
            vmem(NZ, TOK, GRP),
            vmem(NZ, TOK, TOK),
            vmem(NZ, NZ, TOK, dtype=F32),
            vmem(2, NZ, CAP, HALF),
            vmem(2, 2, 4, CAP, HALF),
            vmem(2, 2, 3, CAP, HALF),
            vmem(2, NX, NX, 2, CAP, HALF),
            vmem(D, FFB),
            vmem(D, FFB),
            vmem(2, FFB, HALF),
            vmem(512, FFB, dtype=F32),
            vmem(512, FFB, dtype=F32),
            vmem(512, FFB),
            vmem(NX, NX, 2, CAP, HALF),
            vmem(NX, NX, 2, CAP, HALF),
            vmem(NX, NX, 2, CAP, HALF),
            vmem(NX, 2, CAP, HALF),
            vmem(2, 2, 2, CAP, HALF),
            vmem(2, NX, 2, CAP, HALF),
            vmem(2, NX, 2, CAP, HALF),
            vmem(2, 2, CAP, HALF),
            vmem(2, CAP, HALF),
            vmem(2, 2, CAP, HALF),
            vmem(2, 2, CAP, HALF),
            vmem(CAP, HALF),
            vmem(2, NZ, CAP, HALF),
            vmem(NZ, 2, TOK // 2, GRP),
            vmem(NZ, 8, TOK, dtype=F32),
            vmem(NZ, 8, TOK, dtype=F32),
            vmem(32, TOK, TOK),
            vmem(TOK, TOK, dtype=F32),
            vmem(TOK, D),
            vmem(TOK, D),
            pltpu.SemaphoreType.DMA((N_SEM,)),
            pltpu.SemaphoreType.DMA((N_SEM,)),
            pltpu.SemaphoreType.DMA((12,)),
        ],
        compiler_params=pltpu.CompilerParams(
            collective_id=0, has_side_effects=True, vmem_limit_bytes=60 * 1024 * 1024
        ),
    )(meta, tokens, queries, keys, gate_weight, up_weight, down_weight)


def solution(mesh):
    return jax.shard_map(
        on_device,
        mesh=mesh,
        in_specs=(
            P(("dp", "type"), None),
            P(("dp", "type"), None),
            P("dp", "type", None),
            P(("dp", "type"), None),
            P(("dp", "type"), None),
            P("type", None, "dp"),
            P("type", None, "dp"),
            P("type", "dp", None),
        ),
        out_specs=(P(("dp", "type"), None), P(("dp", "type"), None)),
        check_vma=False,
    )
```

time: 383 us -> 129 us (0.34); the launches traced: 378 us -> 129 us
  waiting for transfers between devices: 284 us -> 0 us
  Pallas kernels: 0 us -> 117 us
  matrix products: 35.1 us -> 0 us
  other arithmetic: 20.7 us -> 1.33 us
  blocking collectives: 16.5 us -> 0 us
  between operations: 13.9 us -> 0.66 us
    all_gather x3 -> x0, waiting for transfers between devices: 164 us -> none  [the longest x1 99.5 us: on_device(): keys_all = lax.all_gather(keys, 'type', axis=0, tiled=True)]
    reduce_scatter x2 -> x0, waiting for transfers between devices: 121 us -> none  [the longest x1 84.7 us: on_device(): lax.psum_scatter(partial_terms.astype(jnp.bfloat16), 'dp', scatter_dimens...]
    pallas_call x0 -> x1, Pallas kernels: none -> 117 us  [on_device(): pl.pallas_call(kernel, out_shape=[jax.ShapeDtypeStruct((TOK, D), BF)] * 2...]
    dot_general x6 -> x0, matrix products: 35.1 us -> none  [the longest x1 11.4 us: on_device(): jnp.einsum('qhd,khd->hqk', query_heads, key_heads, preferred_element_type...]
    sub x2 -> x0, other arithmetic: 18 us -> none  [the longest x1 18 us: on_device(): masked - row_max]
    all_gather x1 -> x0, blocking collectives: 16.5 us -> none  [on_device(): event_types = lax.all_gather(token_types[:, 0], 'type', axis=0, tiled=True)]
    unnamed x10 -> x8, local copies, waits for them, and re-layouts: 4.62 us -> 9.92 us
  transfers between devices with their start and end apart: 5 -> 0, of which waited for: 5 -> 0; matrix products, arithmetic and copies ran while one was open for 8% -> 0% of each run, Pallas kernels for 0% -> 0%
where the time goes in v2:
time: 129 us
  Pallas kernels  117 us (91%)
  local copies, waits for them, and re-layouts  10 us (8%)
  other arithmetic  1.33 us (1%)
    pallas_call x1, Pallas kernels, on_device(): pl.pallas_call(kernel, out_shape=[jax.ShapeDtypeStruct((TOK, D), BF)] * 2...  117 us
    unnamed x8, local copies, waits for them, and re-layouts  9.92 us

profile of v2, /device:TPU:1, one launch (start us, length us, event | category | flops | bytes accessed | tf_op | source)
XLA Modules:
  0.0 128.9 jit_solution(5322504577864551371)
XLA Ops:
  0.6 0.1 pad.7.clone
  0.7 1.3 %fusion.meta_in = s32[8,128]{1,0:T(8,128)} fusion(s32[1,8]{1,0:T(1,128)} %bitcast.2, s32[1,128]{1,0:T(1,128)} %bitcast.3, s32[8]{0:T(128)S(1)} %pad.7.clone), kind=kLoop, calls=%fused_computation.1 | loop fusion | flops 2048 | bytes 4672 | tf_op jit(solution)/shard_map/concatenate | solution.py:453
  2.0 0.0 copy-start
  2.0 4.1 %copy.10.wg_in = bf16[1,4096,224]{2,1,0:T(8,128)(2,1)} copy(bf16[1,4096,224]{1,2,0:T(8,128)(2,1)} %param.13) | data formatting | bytes 3670016 | tf_op args[5]
  6.2 0.0 copy-done
  6.2 2.5 %copy.11.wu_in = bf16[1,4096,224]{2,1,0:T(8,128)(2,1)} copy(bf16[1,4096,224]{1,2,0:T(8,128)(2,1)S(1)} %copy-done) | data formatting | bytes 3670016 | tf_op args[6]
  8.6 116.9 %shard_map.95 = (bf16[128,4096]{1,0:T(8,128)(2,1)}, bf16[128,4096]{1,0:T(8,128)(2,1)}) custom-call(s32[8,128]{1,0:T(8,128)} %fusion.meta_in, bf16[128,4096]{1,0:T(8,128)(2,1)} %tok_in.1, bf16[128,4096]{1,0:T(8,128)(2,1)} %q_in.1, bf16[128,4096]{1,0:T(8,128)(2,1)} %k_in.1, bf16[1,4096,224]{2,1,0:T(8,128)(2,1)} %copy.10.wg_in, ...), custom_call_target="tpu_custom_call" | custom-call | tf_op jit(solution)/shard_map/pallas_call | solution.py:466
  125.5 0.0 copy-start.1
  125.5 2.4 %copy.14 = bf16[128,4096]{1,0:T(8,128)(2,1)} copy(bf16[128,4096]{1,0:T(8,128)(2,1)} %get-tuple-element.4) | data formatting | bytes 2097152
  127.9 0.0 copy-done.1
  127.9 1.0 copy.15
  (1 shorter events, 0.0 us)
Async XLA Ops:
  2.0 4.1 %copy-start = (bf16[1,4096,224]{1,2,0:T(8,128)(2,1)S(1)}, bf16[1,4096,224]{1,2,0:T(8,128)(2,1)}, u32[]{:S(2)}) copy-start(bf16[1,4096,224]{1,2,0:T(8,128)(2,1)} %param.14) | copy-start | bytes 5505028
  125.5 2.4 %copy-start.1 = (bf16[128,4096]{1,0:T(8,128)(2,1)S(1)}, bf16[128,4096]{1,0:T(8,128)(2,1)}, u32[]{:S(2)}) copy-start(bf16[128,4096]{1,0:T(8,128)(2,1)} %get-tuple-element.5) | copy-start | bytes 3145732
